TPU v7x, 32 devices: a whole 2x2x4 slice. The times are simulated.
32 devices in a mesh: group: 2 (over y), tm: 4 (over z), height: 2 (over x), width: 2 (over core).
Axes of the slice: x: 2, y: 2, z: 4, core: 2. Of those that a mesh axis runs over, the one named last changes fastest.
Arguments:
- queries: bfloat16 [8, 16, 32, 1120], P(('group', 'tm'), 'height', 'width'), parts along dimension 0, may hold values from -5 to 5
- attn_keys: bfloat16 [8, 16, 32, 1120], P(('group', 'tm'), 'height', 'width'), parts along dimension 0, may hold values from -40 to 40
- attn_values: bfloat16 [8, 16, 32, 1120], P(('group', 'tm'), 'height', 'width'), parts along dimension 0, may hold values from -7 to 7
- attn_cotangent: bfloat16 [8, 16, 32, 1120], P(('group', 'tm'), 'height', 'width'), parts along dimension 0, may hold values from -7 to 7
- clip_ids: int32 [8], P('group'), parts along dimension 0, may hold values from 0 to 1, as said below
- hidden_pre: bfloat16 [8, 16, 32, 5632], P(('group', 'tm'), 'height', 'width'), parts along dimension 0, may hold values from -6 to 6
- conv_weight: float32 [9, 5632], replicated, may hold values from -2 to 2
Outputs:
- query_grad: bfloat16 [8, 16, 32, 1120], P(('group', 'tm'), 'height', 'width'), parts along dimension 0
- key_grad: bfloat16 [8, 16, 32, 1120], P(('group', 'tm'), 'height', 'width'), parts along dimension 0
- value_gradient: bfloat16 [8, 16, 32, 1120], P(('group', 'tm'), 'height', 'width'), parts along dimension 0
- hidden_grad: bfloat16 [8, 16, 32, 5632], P(('group', 'tm'), 'height', 'width'), parts along dimension 0
There are 2 independent parts, one for each index of `group`. A program takes and returns all parts, laid end to end along the dimension named above; an argument that names none is the same for every part. Nothing has to cross between parts.
Inputs may be any that keep to these rules, and one draw needn't show every extreme that they name: clip_ids never falls; the 4 frames form two clips, 0 then 1, each of 1 to 3 frames.
All inputs are finite; a program needn't handle non-finite values.
Results may differ from a plain program's by a relative error of at most 0.001.
Values may be sent and summed in bfloat16 or wider, within the bound.
No kernel may reach another device: no remote copies, remote signals or barrier semaphores. Data moves between devices by JAX's collectives and lax.ppermute only.
A program may use at most 64 MiB of HBM per device.

v0:
```python
from functools import reduce
import jax
import jax.numpy as jnp
from jax import lax
from jax.sharding import PartitionSpec as P

HEAD_DIM = 112
HEADS = 10
EPSILON = 1e-06
TOP_PRECISION = lax.Precision.HIGHEST


def entering(value, axis, join, neutral, backward):
    count, mine = (lax.axis_size(axis), lax.axis_index(axis))
    pieces = jax.tree.map(lambda part: lax.all_gather(part, axis), value)
    if backward:
        pieces = jax.tree.map(lambda part: part[::-1], pieces)
        mine = count - 1 - mine
    so_far = jax.tree.map(
        lambda part, zero: jnp.full_like(part, 0) + jnp.asarray(zero, part.dtype), value, neutral
    )

    def turn(position, so_far):
        longer = join(so_far, jax.tree.map(lambda part: part[position], pieces))
        return jax.tree.map(lambda new, old: jnp.where(position < mine, new, old), longer, so_far)

    return lax.fori_loop(0, count - 1, turn, so_far)


def padded(block, sides, width):
    for axis, dim in sides:
        count = lax.axis_size(axis)
        forward = [(i, i + 1) for i in range(count - 1)]
        backward = [(target, source) for source, target in forward]
        low = lax.ppermute(
            lax.slice_in_dim(block, block.shape[dim] - width, None, axis=dim), axis, forward
        )
        high = lax.ppermute(lax.slice_in_dim(block, 0, width, axis=dim), axis, backward)
        block = jnp.concatenate([low, block, high], axis=dim)
    return block


def carry_on(earlier, later):
    keeping = 1.0 - later[0]
    return (
        jnp.maximum(earlier[0], later[0]),
        later[1] + keeping * earlier[1],
        later[2] + keeping * earlier[2],
    )


def clip_flags(clip_ids):
    frame = lax.axis_index("tm")
    frame_count = lax.axis_size("tm")
    current = lax.dynamic_index_in_dim(clip_ids, frame, 0, keepdims=False)
    before = lax.dynamic_index_in_dim(clip_ids, jnp.maximum(frame - 1, 0), 0, keepdims=False)
    after = lax.dynamic_index_in_dim(
        clip_ids, jnp.minimum(frame + 1, frame_count - 1), 0, keepdims=False
    )
    starts = jnp.where((frame == 0) | (current != before), 1.0, 0.0).astype(jnp.float32)
    ends = jnp.where((frame == frame_count - 1) | (current != after), 1.0, 0.0).astype(jnp.float32)
    return (starts, ends)


def glu_grad(conv_out, split_at):
    value_part = conv_out[..., :split_at]
    gate_part = conv_out[..., split_at:]
    squash = jax.nn.sigmoid(gate_part)
    glu = value_part * gate_part * squash
    value_gradient = glu * gate_part * squash
    gate_grad = glu * value_part * squash * (1.0 + gate_part * (1.0 - squash))
    return jnp.concatenate([value_gradient, gate_grad], axis=-1)


def depthwise(source, weights, start, sign, height_out, width_out):
    terms = []
    for offset_row in (-1, 0, 1):
        for offset_col in (-1, 0, 1):
            tap_index = (offset_row + 1) * 3 + offset_col + 1
            row_start = start + sign * offset_row
            col_start = start + sign * offset_col
            window = source[
                row_start : row_start + height_out, col_start : col_start + width_out
            ].astype(jnp.float32)
            terms.append(weights[tap_index] * window)
    return reduce(lambda first, second: first + second, terms)


def per_device(queries, attn_keys, attn_values, attn_cotangent, clip_ids, hidden_pre, conv_weight):
    token_count = queries.shape[1] * queries.shape[2]
    flat_width = HEADS * HEAD_DIM
    starts, ends = clip_flags(clip_ids)
    zero_flag = jnp.zeros((), jnp.float32)
    feature_keys = jnp.maximum(attn_keys, 0).reshape(token_count, HEADS, HEAD_DIM)
    value_row_block = attn_values.reshape(token_count, HEADS, HEAD_DIM)
    local_kv = jnp.einsum(
        "jrf,jrx->rfx", feature_keys, value_row_block, preferred_element_type=jnp.float32
    ).reshape(flat_width, HEAD_DIM)
    local_norm = jnp.sum(feature_keys.astype(jnp.float32), axis=0).reshape(flat_width)
    share_kv, share_norm = (
        lax.psum_scatter(local_kv, ("height", "width"), scatter_dimension=0, tiled=True),
        lax.psum_scatter(local_norm, ("height", "width"), scatter_dimension=0, tiled=True),
    )
    earlier = entering(
        (starts, share_kv, share_norm),
        "tm",
        carry_on,
        (zero_flag, jnp.zeros_like(share_kv), jnp.zeros_like(share_norm)),
        False,
    )
    part_kv = share_kv + (1.0 - starts) * earlier[1]
    part_norm = share_norm + (1.0 - starts) * earlier[2]
    state_key_value, state_norm = (
        lax.all_gather(part_kv, ("height", "width"), axis=0, tiled=True),
        lax.all_gather(part_norm, ("height", "width"), axis=0, tiled=True),
    )
    state_key_value = state_key_value.reshape(HEADS, HEAD_DIM, HEAD_DIM)
    state_norm = state_norm.reshape(HEADS, HEAD_DIM)
    feature_query = (
        jnp.maximum(queries, 0).reshape(token_count, HEADS, HEAD_DIM).astype(jnp.float32)
    )
    cotangent = attn_cotangent.reshape(token_count, HEADS, HEAD_DIM).astype(jnp.float32)
    ratio_numerator = jnp.einsum(
        "cob,obq->coq", feature_query, state_key_value, precision=TOP_PRECISION
    )
    denominator = (
        jnp.einsum("thk,hk->th", feature_query, state_norm, precision=TOP_PRECISION) + EPSILON
    )
    attended = ratio_numerator / denominator[..., None]
    scaled_gradient = cotangent / denominator[..., None]
    denominator_grad = -jnp.sum(cotangent * attended, axis=-1) / denominator
    query_feature_gradient = jnp.einsum(
        "dla,lja->dlj", scaled_gradient, state_key_value, precision=TOP_PRECISION
    )
    query_feature_gradient = query_feature_gradient + state_norm[None] * denominator_grad[..., None]
    query_grad = (
        jnp.where(feature_query > 0.0, query_feature_gradient, 0.0)
        .reshape(queries.shape)
        .astype(jnp.bfloat16)
    )
    gradient_key_value = jnp.einsum(
        "jrf,jrx->rfx", feature_query, scaled_gradient, precision=TOP_PRECISION
    ).reshape(flat_width, HEAD_DIM)
    grad_norm = jnp.einsum(
        "thk,th->hk", feature_query, denominator_grad, precision=TOP_PRECISION
    ).reshape(flat_width)
    share_grad_kv, share_grad_norm = (
        lax.psum_scatter(gradient_key_value, ("height", "width"), scatter_dimension=0, tiled=True),
        lax.psum_scatter(grad_norm, ("height", "width"), scatter_dimension=0, tiled=True),
    )
    later = entering(
        (ends, share_grad_kv, share_grad_norm),
        "tm",
        carry_on,
        (zero_flag, jnp.zeros_like(share_grad_kv), jnp.zeros_like(share_grad_norm)),
        True,
    )
    part_grad_kv = share_grad_kv + (1.0 - ends) * later[1]
    part_grad_norm = share_grad_norm + (1.0 - ends) * later[2]
    total_key_value, norm_total = (
        lax.all_gather(part_grad_kv, ("height", "width"), axis=0, tiled=True),
        lax.all_gather(part_grad_norm, ("height", "width"), axis=0, tiled=True),
    )
    total_key_value = total_key_value.reshape(HEADS, HEAD_DIM, HEAD_DIM)
    norm_total = norm_total.reshape(HEADS, HEAD_DIM)
    key_feat_grad = (
        jnp.einsum(
            "dla,lja->dlj",
            value_row_block.astype(jnp.float32),
            total_key_value,
            precision=TOP_PRECISION,
        )
        + norm_total[None]
    )
    key_grad = (
        jnp.where(feature_keys > 0, key_feat_grad, 0.0)
        .reshape(attn_keys.shape)
        .astype(jnp.bfloat16)
    )
    value_gradient = jnp.einsum(
        "cob,obq->coq", feature_keys.astype(jnp.float32), total_key_value, precision=TOP_PRECISION
    )
    value_gradient = value_gradient.reshape(attn_values.shape).astype(jnp.bfloat16)
    row_count = hidden_pre.shape[1]
    col_count = hidden_pre.shape[2]
    split_at = hidden_pre.shape[3] // 2
    widened = padded(hidden_pre, (("height", 1), ("width", 2)), 2)[0]
    conv_out = depthwise(widened, conv_weight, 1, 1, row_count + 2, col_count + 2)
    row_global = lax.axis_index("height") * row_count + jnp.arange(row_count + 2) - 1
    col_global = lax.axis_index("width") * col_count + jnp.arange(col_count + 2) - 1
    row_inside = (row_global >= 0) & (row_global < row_count * lax.axis_size("height"))
    col_inside = (col_global >= 0) & (col_global < col_count * lax.axis_size("width"))
    inside = (row_inside[:, None] & col_inside[None, :]).astype(jnp.float32)
    conv_grad = glu_grad(conv_out, split_at) * inside[:, :, None]
    hidden_grad = depthwise(conv_grad, conv_weight, 1, -1, row_count, col_count)
    hidden_grad = hidden_grad[None].astype(jnp.bfloat16)
    return (query_grad, key_grad, value_gradient, hidden_grad)


def solution(mesh):
    return jax.shard_map(
        per_device,
        mesh=mesh,
        in_specs=(
            P(("group", "tm"), "height", "width", None),
            P(("group", "tm"), "height", "width", None),
            P(("group", "tm"), "height", "width", None),
            P(("group", "tm"), "height", "width", None),
            P("group"),
            P(("group", "tm"), "height", "width", None),
            P(),
        ),
        out_specs=(
            P(("group", "tm"), "height", "width", None),
            P(("group", "tm"), "height", "width", None),
            P(("group", "tm"), "height", "width", None),
            P(("group", "tm"), "height", "width", None),
        ),
        check_vma=False,
    )
```

profile of v0, /device:TPU:0, one launch (start us, length us, event | category | flops | bytes accessed | tf_op | source)
XLA Modules:
  0.0 199.7 jit_solution(10173100332461614557)
XLA Ops:
  7.2 1.9 fusion.27
  9.1 5.7 %collective-permute-start = (bf16[1,2,16,5632]{3,2,1,0:T(8,128)(2,1)S(1)}, bf16[1,2,16,5632]{3,2,1,0:T(8,128)(2,1)}, u32[]{:S(2)}, u32[]{:S(2)}) collective-permute-start(bf16[1,2,16,5632]{3,2,1,0:T(8,128)(2,1)S(1)} %get-tuple-element.356), channel_id=1, source_target_pairs={{0,2},{1,3},{4,6},{5,7},{8,10},{9,11},{12,14},{13,15},{16,18},{17,... | collective-permute-start | bytes 1081352 | tf_op jit(solution)/shard_map/ppermute | solution.py:35
  14.8 1.4 collective-permute-start.1
  19.3 1.2 fusion.30
  21.8 8.0 %all-reduce.7 = f32[1120]{0:T(1024)S(1)} all-reduce(f32[1120]{0:T(1024)S(1)} %convert_reduce_fusion), channel_id=7, replica_groups=mesh['group'=2,'tm'=4,'height'=2,'width'=2] {'height','width'}, use_global_device_ids=true, to_apply=%region_2.3.clone | all-reduce | flops 1120 | bytes 8960
  36.7 1.5 constant_dynamic-update-slice_fusion.1
  39.2 1.2 fusion.26
  40.4 2.0 collective-permute-start.2
  42.4 1.3 collective-permute-start.3
  44.3 12.9 %all-reduce.11 = (f32[4]{0:T(128)}, f32[1120]{0:T(1024)S(1)}) all-reduce(f32[4]{0:T(128)S(1)} %dynamic-update-slice, f32[1120]{0:T(1024)S(1)} %dynamic-slice_dynamic-update-slice_fusion.1), channel_id=1, replica_groups=mesh['group'=2,'tm'=4,'height'=2,'width'=2] {'tm'}, use_global_device_ids=true, to_apply=%add | all-reduce | flops 1124 | bytes 8992
  57.9 2.4 %reshape.147 = bf16[128,10,112]{2,1,0:T(8,128)(2,1)} reshape(bf16[1,8,16,1120]{3,2,1,0:T(8,128)(2,1)} %broadcast_maximum_fusion.1) | data formatting | bytes 573440 | tf_op jit(solution)/shard_map/reshape | solution.py:120
  60.2 1.4 copy.36
  61.6 2.5 %reshape.156 = f32[128,10,112]{2,1,0:T(8,128)} reshape(bf16[1,8,16,1120]{3,2,1,0:T(8,128)(2,1)} %param.14) | data formatting | bytes 860160 | tf_op jit(solution)/shard_map/convert_element_type | solution.py:122
  64.1 2.3 %copy.39 = f32[128,10,112]{0,2,1:T(8,128)} copy(f32[128,10,112]{2,1,0:T(8,128)} %reshape.156) | data formatting | bytes 1146880 | tf_op jit(solution)/shard_map/convert_element_type | solution.py:122
  68.3 1.8 dynamic-update-slice.3
  70.8 2.4 %maximum_bitcast_fusion = bf16[12,20,5632]{2,1,0:T(8,128)(2,1)S(1)} fusion(bf16[1,12,2,5632]{3,2,1,0:T(2,128)(2,1)} %collective-permute-done.3, bf16[1,12,16,5632]{3,2,1,0:T(8,128)(2,1)S(1)} %constant_dynamic-update-slice_fusion, bf16[1,12,2,5632]{3,2,1,0:T(2,128)(2,1)} %collective-permute-done.2), kind=kLoop, calls=%fused_computation.10 | loop fusion | flops 8110080 | bytes 5406720 | tf_op jit(solution)/shard_map/squeeze | solution.py:187
  73.2 5.8 %multiply_add_fusion = f32[10,18,5632]{2,1,0:T(8,128)S(1)} fusion(bf16[12,20,5632]{2,1,0:T(8,128)(2,1)S(1)} %maximum_bitcast_fusion, f32[5632]{0:T(1024)S(1)} %get-tuple-element.317, f32[5632]{0:T(1024)S(1)} %get-tuple-element.318, f32[5632]{0:T(1024)S(1)} %get-tuple-element.311, f32[5632]{0:T(1024)S(1)} %get-tuple-element.312, ...), kind=kLoop, calls=%fused_computation.9 | loop fusion | flops 26357760 | bytes 22505472 | tf_op jit(solution)/shard_map/add | solution.py:86
  79.1 1.4 multiply_multiply_fusion
  80.5 3.0 %maximum_multiply_fusion = f32[10,18,5632]{2,1,0:T(8,128)} fusion(f32[10,18,2816]{2,1,0:T(8,128)S(1)} %get-tuple-element.352, f32[10,18,2816]{2,1,0:T(8,128)S(1)} %get-tuple-element.351, f32[10,18]{1,0:T(8,128)S(1)} %and_convert_fusion), kind=kLoop, calls=%fused_computation.8 | loop fusion | flops 2027520 | bytes 8110800 | tf_op jit(solution)/shard_map/mul | solution.py:194
  83.5 16.9 %all-gather = f32[1120,112]{1,0:T(8,128)S(1)} all-gather(f32[280,112]{1,0:T(8,128)} %reduce-scatter.7.cloned.1.call-done), channel_id=2, replica_groups=mesh['group'=2,'tm'=4,'height'=2,'width'=2] {'tm'}, dimensions={0}, use_global_device_ids=true | all-gather | bytes 627200 | tf_op jit(solution)/shard_map/all_gather | solution.py:15
  100.4 4.1 %while.32 = (s32[]{:T(128)}, f32[280,112]{1,0:T(8,128)S(1)}, f32[280]{0:T(512)S(1)}, s32[]{:T(128)}, f32[4,280,112]{2,1,0:T(8,128)S(1)}, /*index=5*/f32[4]{0:T(1...) while((s32[]{:T(128)}, f32[280,112]{1,0:T(8,128)S(1)}, f32[280]{0:T(512)S(1)}, ...), condition=%wide.region_4.5_spmd.clone, body=%wide.region_3.4_spmd.clone.sunk | while | flops 126565 | bytes 382083 | solution.py:27
  104.8 5.7 %all-reduce.2 = f32[1120]{0:T(1024)S(1)} all-reduce(f32[1120]{0:T(1024)S(1)} %add_dynamic-update-slice_fusion.1), channel_id=1, replica_groups=mesh['group'=2,'tm'=4,'height'=2,'width'=2] {'height','width'}, use_global_device_ids=true, to_apply=%add.2 | all-reduce | flops 1120 | bytes 8960
  110.9 1.6 fusion.22
  112.6 7.9 %all_gather.54 = f32[1120,112]{1,0:T(8,128)S(1)} all-gather(f32[280,112]{1,0:T(8,128)S(1)} %multiply_add_fusion.2), channel_id=1, replica_groups=mesh['group'=2,'tm'=4,'height'=2,'width'=2] {'height','width'}, dimensions={0}, use_global_device_ids=true | all-gather | bytes 627200 | tf_op jit(solution)/shard_map/all_gather | solution.py:114
  121.8 6.7 %all-reduce.9 = f32[1120]{0:T(1024)S(1)} all-reduce(f32[1120]{0:T(1024)S(1)} %reshape.154), channel_id=9, replica_groups=mesh['group'=2,'tm'=4,'height'=2,'width'=2] {'height','width'}, use_global_device_ids=true, to_apply=%region_7.8.clone | all-reduce | flops 1120 | bytes 8960
  128.6 14.8 %fusion.11 = bf16[1,8,16,5632]{3,2,1,0:T(8,128)(2,1)} fusion(f32[10,18,5632]{2,1,0:T(8,128)} %maximum_multiply_fusion, f32[5632]{0:T(1024)S(1)} %get-tuple-element.317, f32[5632]{0:T(1024)S(1)} %get-tuple-element.318, f32[5632]{0:T(1024)S(1)} %get-tuple-element.311, f32[5632]{0:T(1024)S(1)} %get-tuple-element.312, f32[5632]{0:T(1024)S(1)} %get-tuple-element.313, ...), kind=kLoop, calls=%fused_computation.33 | loop fusion | flops 12976128 | bytes 27596800 | tf_op jit(solution)/shard_map/convert_element_type | solution.py:196
  143.4 9.0 %all-reduce.10 = (f32[4]{0:T(128)S(1)}, f32[1120]{0:T(1024)S(1)}) all-reduce(f32[4]{0:T(128)S(1)} %copy-done.9, f32[1120]{0:T(1024)S(1)} %dynamic-slice_dynamic-update-slice_fusion), channel_id=1, replica_groups=mesh['group'=2,'tm'=4,'height'=2,'width'=2] {'tm'}, use_global_device_ids=true, to_apply=%add.3 | all-reduce | flops 1124 | bytes 8992
  154.0 1.1 convert_element_type.105
  155.1 15.5 %all-gather.2 = f32[1120,112]{1,0:T(8,128)S(1)} all-gather(f32[280,112]{1,0:T(8,128)} %reduce-scatter.9.cloned.1.call-done), channel_id=4, replica_groups=mesh['group'=2,'tm'=4,'height'=2,'width'=2] {'tm'}, dimensions={0}, use_global_device_ids=true | all-gather | bytes 627200 | tf_op jit(solution)/shard_map/all_gather | solution.py:15
  170.6 4.1 %while.33 = (s32[]{:T(128)}, f32[280,112]{1,0:T(8,128)S(1)}, f32[280]{0:T(512)S(1)}, s32[]{:T(128)}, f32[4,280,112]{2,1,0:T(8,128)S(1)}, /*index=5*/f32[4]{0:T(1...) while((s32[]{:T(128)}, f32[280,112]{1,0:T(8,128)S(1)}, f32[280]{0:T(512)S(1)}, ...), condition=%wide.region_9.10_spmd.clone, body=%wide.region_8.9_spmd.clone.sunk | while | flops 126565 | bytes 382083 | solution.py:27
  174.8 6.9 %all_gather.62 = f32[1120,112]{1,0:T(8,128)S(1)} all-gather(f32[280,112]{1,0:T(8,128)S(1)} %multiply_add_fusion.1), channel_id=1, replica_groups=mesh['group'=2,'tm'=4,'height'=2,'width'=2] {'height','width'}, dimensions={0}, use_global_device_ids=true | all-gather | bytes 627200 | tf_op jit(solution)/shard_map/all_gather | solution.py:161
  184.0 6.8 %all-reduce.5 = f32[1120]{0:T(1024)S(1)} all-reduce(f32[1120]{0:T(1024)S(1)} %add_dynamic-update-slice_fusion), channel_id=1, replica_groups=mesh['group'=2,'tm'=4,'height'=2,'width'=2] {'height','width'}, use_global_device_ids=true, to_apply=%add.5 | all-reduce | flops 1120 | bytes 8960
  (114 shorter events, 24.0 us)
Async XLA Ops:
  7.2 11.1 %copy-start.4 = (bf16[1,8,16,1120]{3,2,1,0:T(8,128)(2,1)S(1)}, bf16[1,8,16,1120]{3,2,1,0:T(8,128)(2,1)}, u32[]{:S(2)}) copy-start(bf16[1,8,16,1120]{3,2,1,0:T(8,128)(2,1)} %param.13) | copy-start | bytes 860164
  7.2 76.3 %reduce-scatter.7.cloned.1.call-start = ((), (), s32[]{:S(2)}) async-start(), calls=%async_computation.2 | async-start | bytes 716800
  9.1 11.5 %copy-start = (bf16[1,8,16,1120]{3,2,1,0:T(8,128)(2,1)S(1)}, bf16[1,8,16,1120]{3,2,1,0:T(8,128)(2,1)}, u32[]{:S(2)}) copy-start(bf16[1,8,16,1120]{3,2,1,0:T(8,128)(2,1)} %param.12) | copy-start | bytes 860164
  9.1 26.6 %collective-permute-start = (bf16[1,2,16,5632]{3,2,1,0:T(8,128)(2,1)S(1)}, bf16[1,2,16,5632]{3,2,1,0:T(8,128)(2,1)}, u32[]{:S(2)}, u32[]{:S(2)}) collective-permute-start(bf16[1,2,16,5632]{3,2,1,0:T(8,128)(2,1)S(1)} %get-tuple-element.356), channel_id=1, source_target_pairs={{0,2},{1,3},{4,6},{5,7},{8,10},{9,11},{12,14},{13,15},{16,18},{17,... | collective-permute-start | bytes 1081352 | tf_op jit(solution)/shard_map/ppermute | solution.py:35
  14.8 5.8 %copy-start.6 = (f32[9,5632]{1,0:T(8,128)S(1)}, f32[9,5632]{1,0:T(8,128)}, u32[]{:S(2)}) copy-start(f32[9,5632]{1,0:T(8,128)} %param.17) | copy-start | bytes 608260
  14.8 23.4 %collective-permute-start.1 = (bf16[1,2,16,5632]{3,2,1,0:T(8,128)(2,1)}, bf16[1,2,16,5632]{3,2,1,0:T(8,128)(2,1)}, u32[]{:S(2)}, u32[]{:S(2)}) collective-permute-start(bf16[1,2,16,5632]{3,2,1,0:T(8,128)(2,1)} %get-tuple-element.355), channel_id=1, source_target_pairs={{2,0},{3,1},{6,4},{7,5},{10,8},{11,9},{14,12},{15,13},{18,16},{19,... | collective-permute-start | bytes 1081352 | tf_op jit(solution)/shard_map/ppermute | solution.py:38
  17.2 12.5 %copy-start.7 = (s32[4]{0:T(128)S(1)}, s32[4]{0:T(128)}, u32[]{:S(2)}) copy-start(s32[4]{0:T(128)} %param.15) | copy-start | bytes 52
  17.3 14.5 %copy-start.11 = (u32[32]{0:T(128)S(1)}, u32[32]{0:T(128)}, u32[]{:S(2)}) copy-start(u32[32]{0:T(128)} %constant.120) | copy-start | bytes 388
  17.3 15.1 %copy-start.8 = (u32[32]{0:T(128)S(1)}, u32[32]{0:T(128)}, u32[]{:S(2)}) copy-start(u32[32]{0:T(128)} %constant.130) | copy-start | bytes 388
  17.3 17.7 %copy-start.5 = (bf16[1,8,16,1120]{3,2,1,0:T(8,128)(2,1)S(1)}, bf16[1,8,16,1120]{3,2,1,0:T(8,128)(2,1)}, u32[]{:S(2)}) copy-start(bf16[1,8,16,1120]{3,2,1,0:T(8,128)(2,1)} %param.11) | copy-start | bytes 860164
  20.5 134.6 %reduce-scatter.9.cloned.1.call-start = ((), (), s32[]{:S(2)}) async-start(), calls=%async_computation.3 | async-start | bytes 716800
  40.4 30.4 %collective-permute-start.2 = (bf16[1,12,2,5632]{3,2,1,0:T(2,128)(2,1)}, bf16[1,12,2,5632]{3,2,1,0:T(2,128)(2,1)}, u32[]{:S(2)}, u32[]{:S(2)}) collective-permute-start(bf16[1,12,2,5632]{3,2,1,0:T(2,128)(2,1)} %get-tuple-element.353), channel_id=1, source_target_pairs={{0,1},{2,3},{4,5},{6,7},{8,9},{10,11},{12,13},{14,15},{16,17},{18,... | collective-permute-start | bytes 811016 | tf_op jit(solution)/shard_map/ppermute | solution.py:35
  42.4 28.4 %collective-permute-start.3 = (bf16[1,12,2,5632]{3,2,1,0:T(2,128)(2,1)}, bf16[1,12,2,5632]{3,2,1,0:T(2,128)(2,1)}, u32[]{:S(2)}, u32[]{:S(2)}) collective-permute-start(bf16[1,12,2,5632]{3,2,1,0:T(2,128)(2,1)} %get-tuple-element.354), channel_id=1, source_target_pairs={{1,0},{3,2},{5,4},{7,6},{9,8},{11,10},{13,12},{15,14},{17,16},{19,... | collective-permute-start | bytes 811016 | tf_op jit(solution)/shard_map/ppermute | solution.py:38
  80.5 20.0 %copy-start.10 = (f32[4]{0:T(128)S(1)}, f32[4]{0:T(128)}, u32[]{:S(2)}) copy-start(f32[4]{0:T(128)} %get-tuple-element.453) | copy-start | bytes 52
  83.5 27.4 %copy-start.1 = (f32[128,10,112]{0,2,1:T(8,128)S(1)}, f32[128,10,112]{0,2,1:T(8,128)}, u32[]{:S(2)}) copy-start(f32[128,10,112]{0,2,1:T(8,128)} %copy.39) | copy-start | bytes 1720324
  100.4 12.1 %copy-start.2 = (f32[280,112]{1,0:T(8,128)S(1)}, f32[280,112]{1,0:T(8,128)}, u32[]{:S(2)}) copy-start(f32[280,112]{1,0:T(8,128)} %reduce-scatter.7.cloned.1.call-done) | copy-start | bytes 376324
  128.6 14.8 %copy-start.9 = (f32[4]{0:T(128)S(1)}, f32[4]{0:T(128)}, u32[]{:S(2)}) copy-start(f32[4]{0:T(128)} %dynamic-update-slice.3) | copy-start | bytes 52
  155.1 19.6 %copy-start.3 = (f32[280,112]{1,0:T(8,128)S(1)}, f32[280,112]{1,0:T(8,128)}, u32[]{:S(2)}) copy-start(f32[280,112]{1,0:T(8,128)} %reduce-scatter.9.cloned.1.call-done) | copy-start | bytes 376324
Sparse Core Ops, SparseCore 0:
  20.6 25.0 reduce-scatter.6
  112.7 20.6 reduce-scatter.8
where the time goes:
time: 201 us; the launch traced here: 200 us
  blocking collectives  96.2 us (48%)
  other arithmetic  32 us (16%)
  local copies, waits for them, and re-layouts  31.9 us (16%)
  between operations  18.9 us (9%)
  starting transfers between devices  10.5 us (5%)
  matrix products  6.22 us (3%)
  loops' own time  4.06 us (2%)
    unnamed x6, blocking collectives  49 us
    all_gather x2, blocking collectives, entering(): pieces = jax.tree.map(lambda part: lax.all_gather(part, axis), value)  32.4 us
    convert_element_type x1, other arithmetic, per_device(): hidden_grad = hidden_grad[None].astype(jnp.bfloat16)  14.8 us
    all_gather x1, blocking collectives, per_device(): lax.all_gather(part_kv, ('height', 'width'), axis=0, tiled=True)  7.86 us
    ppermute x2, starting transfers between devices, padded(): lax.ppermute(lax.slice_in_dim(block, block.shape[dim] - width, None, axis...  7.68 us
    unnamed x38, local copies, waits for them, and re-layouts  7.01 us
    all_gather x1, blocking collectives, per_device(): lax.all_gather(part_grad_kv, ('height', 'width'), axis=0, tiled=True)  6.9 us
    add x1, other arithmetic, depthwise(): return reduce(lambda first, second: first + second, terms)  5.8 us
  transfers between devices with their start and end apart: 6, of which 0 were waited for; matrix products, arithmetic and copies ran while one was open for 29% of the time, Pallas kernels for 0%

commit v1 on v0

--- a/solution.py
+++ b/solution.py
@@ -8,6 +8,37 @@
 HEADS = 10
 EPSILON = 1e-06
 TOP_PRECISION = lax.Precision.HIGHEST
+
+
+def do_slot_here(original, device_axis):
+    now, x_new, moved = (
+        lax.psum(1, axis_name=device_axis),
+        lax.axis_index(device_axis),
+        original.shape[0],
+    )
+    val2 = lax.dynamic_update_slice_in_dim(
+        jnp.zeros(
+            [dev_i * now if u == 0 else dev_i for u, dev_i in enumerate(original.shape)],
+            original.dtype,
+        ),
+        original,
+        x_new * moved,
+        axis=0,
+    )
+    parts_out = side_arr = original
+    for k in tuple(range(1, now // 2 + 1)):
+        parts_out = lax.ppermute(
+            parts_out, axis_name=device_axis, perm=[(u, (u + 1) % now) for u in range(now)]
+        )
+        val2 = lax.dynamic_update_slice_in_dim(val2, parts_out, (x_new - k) % now * moved, axis=0)
+        if 2 * k < now:
+            side_arr = lax.ppermute(
+                side_arr, axis_name=device_axis, perm=[(u, (u - 1) % now) for u in range(now)]
+            )
+            val2 = lax.dynamic_update_slice_in_dim(
+                val2, side_arr, (x_new + k) % now * moved, axis=0
+            )
+    return val2
 
 
 def entering(value, axis, join, neutral, backward):
@@ -111,7 +142,7 @@
     part_kv = share_kv + (1.0 - starts) * earlier[1]
     part_norm = share_norm + (1.0 - starts) * earlier[2]
     state_key_value, state_norm = (
-        lax.all_gather(part_kv, ("height", "width"), axis=0, tiled=True),
+        do_slot_here(part_kv, ("height", "width")),
         lax.all_gather(part_norm, ("height", "width"), axis=0, tiled=True),
     )
     state_key_value = state_key_value.reshape(HEADS, HEAD_DIM, HEAD_DIM)

time: 201 us -> 192 us (0.955)
  other arithmetic: 32 us -> 18.6 us
  waiting for transfers between devices: 0.05 us -> 4.5 us
  blocking collectives: 96.2 us -> 92.1 us
  starting transfers between devices: 10.5 us -> 14.2 us
    convert_element_type x1, other arithmetic: 14.8 us -> 3.73 us  [per_device(): hidden_grad = hidden_grad[None].astype(jnp.bfloat16)]
    all_gather x1 -> x0, blocking collectives: 7.86 us -> none  [per_device(): lax.all_gather(part_kv, ('height', 'width'), axis=0, tiled=True)]
    ppermute x0 -> x3, waiting for transfers between devices: none -> 4.46 us  [the longest x2 4.45 us: do_slot_here(): lax.ppermute(parts_out, axis_name=device_axis, perm=[(u, (u + 1) % now) f...]
    unnamed x6, blocking collectives: 49 us -> 51.6 us
    mul x1, other arithmetic: 3.04 us -> 0.62 us  [per_device(): conv_grad = glu_grad(conv_out, split_at) * inside[:, :, None]]
    ppermute x2, starting transfers between devices: 7.68 us -> 9.73 us  [padded(): lax.ppermute(lax.slice_in_dim(block, block.shape[dim] - width, None, axis...]
    unnamed x38 -> x36, local copies, waits for them, and re-layouts: 7.01 us -> 7.31 us
  transfers between devices with their start and end apart: 6 -> 9, of which waited for: 0 -> 1; matrix products, arithmetic and copies ran while one was open for 29% -> 23% of each run, Pallas kernels for 0% -> 0%
where the time goes in v1:
time: 192 us
  blocking collectives  92.1 us (48%)
  local copies, waits for them, and re-layouts  33 us (17%)
  between operations  19.1 us (10%)
  other arithmetic  18.6 us (10%)
  starting transfers between devices  14.2 us (7%)
  matrix products  6.12 us (3%)
  waiting for transfers between devices  4.5 us (2%)
  loops' own time  4.06 us (2%)
    unnamed x6, blocking collectives  51.6 us
    all_gather x2, blocking collectives, entering(): pieces = jax.tree.map(lambda part: lax.all_gather(part, axis), value)  33.6 us
    ppermute x2, starting transfers between devices, padded(): lax.ppermute(lax.slice_in_dim(block, block.shape[dim] - width, None, axis...  9.73 us
    unnamed x36, local copies, waits for them, and re-layouts  7.31 us
    all_gather x1, blocking collectives, per_device(): lax.all_gather(part_grad_kv, ('height', 'width'), axis=0, tiled=True)  6.9 us
    add x1, other arithmetic, depthwise(): return reduce(lambda first, second: first + second, terms)  5.79 us
    convert_element_type x2, local copies, waits for them, and re-layouts, per_device(): attn_cotangent.reshape(token_count, HEADS, HEAD_DIM).astype(jnp.float32)  4.82 us
    ppermute x2, waiting for transfers between devices, do_slot_here(): lax.ppermute(parts_out, axis_name=device_axis, perm=[(u, (u + 1) % now) f...  4.45 us
  transfers between devices with their start and end apart: 9, of which 1 were waited for; matrix products, arithmetic and copies ran while one was open for 23% of the time, Pallas kernels for 0%

profile of v1, /device:TPU:0, one launch (start us, length us, event | category | flops | bytes accessed | tf_op | source)
XLA Modules:
  0.0 191.6 jit_solution(4269447907719446334)
XLA Ops:
  9.4 1.6 reshape.149
  11.4 1.1 fusion.30
  13.4 5.6 %collective-permute-start.3 = (bf16[1,2,16,5632]{3,2,1,0:T(8,128)(2,1)S(1)}, bf16[1,2,16,5632]{3,2,1,0:T(8,128)(2,1)}, u32[]{:S(2)}, u32[]{:S(2)}) collective-permute-start(bf16[1,2,16,5632]{3,2,1,0:T(8,128)(2,1)S(1)} %get-tuple-element.358), channel_id=1, source_target_pairs={{0,2},{1,3},{4,6},{5,7},{8,10},{9,11},{12,14},{13,15},{16,18},{17,... | collective-permute-start | bytes 1081352 | tf_op jit(solution)/shard_map/ppermute | solution.py:66
  19.0 1.3 collective-permute-start.4
  20.4 10.1 %all-reduce.7 = f32[1120]{0:T(1024)S(1)} all-reduce(f32[1120]{0:T(1024)S(1)} %convert_reduce_fusion), channel_id=7, replica_groups=mesh['group'=2,'tm'=4,'height'=2,'width'=2] {'height','width'}, use_global_device_ids=true, to_apply=%region_2.3.clone | all-reduce | flops 1120 | bytes 8960
  30.5 2.3 %slice_reduce_fusion.8 = (f32[5632]{0:T(1024)S(1)}, f32[5632]{0:T(1024)S(1)}, f32[5632]{0:T(1024)S(1)}, f32[5632]{0:T(1024)S(1)}, f32[5632]{0:T(1024)S(1)}, /*in...) fusion(f32[9,5632]{1,0:T(8,128)} %param.17), kind=kLoop, calls=%fused_computation.64 | loop fusion | bytes 405504 | tf_op jit(solution)/shard_map/slice | solution.py:116
  40.6 1.5 constant_dynamic-update-slice_fusion.1
  42.1 1.2 fusion.26
  43.3 4.2 %collective-permute-start.5 = (bf16[1,12,2,5632]{3,2,1,0:T(2,128)(2,1)}, bf16[1,12,2,5632]{3,2,1,0:T(2,128)(2,1)}, u32[]{:S(2)}, u32[]{:S(2)}) collective-permute-start(bf16[1,12,2,5632]{3,2,1,0:T(2,128)(2,1)} %get-tuple-element.355), channel_id=1, source_target_pairs={{0,1},{2,3},{4,5},{6,7},{8,9},{10,11},{12,13},{14,15},{16,17},{18,... | collective-permute-start | bytes 811016 | tf_op jit(solution)/shard_map/ppermute | solution.py:66
  47.5 1.3 collective-permute-start.6
  49.3 13.1 %all-reduce.11 = (f32[4]{0:T(128)}, f32[1120]{0:T(1024)S(1)}) all-reduce(f32[4]{0:T(128)S(1)} %dynamic-update-slice, f32[1120]{0:T(1024)S(1)} %dynamic-slice_dynamic-update-slice_fusion.1), channel_id=1, replica_groups=mesh['group'=2,'tm'=4,'height'=2,'width'=2] {'tm'}, use_global_device_ids=true, to_apply=%add | all-reduce | flops 1124 | bytes 8992
  63.2 2.4 %reshape.147 = bf16[128,10,112]{2,1,0:T(8,128)(2,1)} reshape(bf16[1,8,16,1120]{3,2,1,0:T(8,128)(2,1)} %broadcast_maximum_fusion.1) | data formatting | bytes 573440 | tf_op jit(solution)/shard_map/reshape | solution.py:151
  65.6 1.4 copy.36
  67.0 2.5 %reshape.156 = f32[128,10,112]{2,1,0:T(8,128)} reshape(bf16[1,8,16,1120]{3,2,1,0:T(8,128)(2,1)} %param.14) | data formatting | bytes 860160 | tf_op jit(solution)/shard_map/convert_element_type | solution.py:153
  69.5 2.3 %copy.39 = f32[128,10,112]{0,2,1:T(8,128)} copy(f32[128,10,112]{2,1,0:T(8,128)} %reshape.156) | data formatting | bytes 1146880 | tf_op jit(solution)/shard_map/convert_element_type | solution.py:153
  73.6 1.9 dynamic-update-slice.3
  76.3 2.4 %maximum_bitcast_fusion = bf16[12,20,5632]{2,1,0:T(8,128)(2,1)S(1)} fusion(bf16[1,12,2,5632]{3,2,1,0:T(2,128)(2,1)} %collective-permute-done.6, bf16[1,12,16,5632]{3,2,1,0:T(8,128)(2,1)S(1)} %constant_dynamic-update-slice_fusion, bf16[1,12,2,5632]{3,2,1,0:T(2,128)(2,1)} %collective-permute-done.5), kind=kLoop, calls=%fused_computation.10 | loop fusion | flops 8110080 | bytes 5406720 | tf_op jit(solution)/shard_map/squeeze | solution.py:218
  78.7 5.8 %multiply_add_fusion = f32[10,18,5632]{2,1,0:T(8,128)S(1)} fusion(bf16[12,20,5632]{2,1,0:T(8,128)(2,1)S(1)} %maximum_bitcast_fusion, f32[5632]{0:T(1024)S(1)} %get-tuple-element.317, f32[5632]{0:T(1024)S(1)} %get-tuple-element.318, f32[5632]{0:T(1024)S(1)} %get-tuple-element.311, f32[5632]{0:T(1024)S(1)} %get-tuple-element.312, ...), kind=kLoop, calls=%fused_computation.9 | loop fusion | flops 26357760 | bytes 22505472 | tf_op jit(solution)/shard_map/add | solution.py:117
  84.5 1.4 multiply_multiply_fusion
  86.5 3.7 %fusion.11 = bf16[1,8,16,5632]{3,2,1,0:T(8,128)(2,1)} fusion(f32[10,18,5632]{2,1,0:T(8,128)S(1)} %maximum_multiply_fusion, f32[5632]{0:T(1024)S(1)} %get-tuple-element.317, f32[5632]{0:T(1024)S(1)} %get-tuple-element.318, f32[5632]{0:T(1024)S(1)} %get-tuple-element.311, f32[5632]{0:T(1024)S(1)} %get-tuple-element.312, f32[5632]{0:T(1024)S(1)} %get-tuple-element.313, ...), kind=kLoop, calls=%fused_computation.33 | loop fusion | flops 12976128 | bytes 27596800 | tf_op jit(solution)/shard_map/convert_element_type | solution.py:227
  90.3 16.9 %all-gather = f32[1120,112]{1,0:T(8,128)S(1)} all-gather(f32[280,112]{1,0:T(8,128)} %reduce-scatter.7.cloned.1.call-done), channel_id=2, replica_groups=mesh['group'=2,'tm'=4,'height'=2,'width'=2] {'tm'}, dimensions={0}, use_global_device_ids=true | all-gather | bytes 627200 | tf_op jit(solution)/shard_map/all_gather | solution.py:46
  107.2 4.1 %while.32 = (s32[]{:T(128)}, f32[280,112]{1,0:T(8,128)S(1)}, f32[280]{0:T(512)S(1)}, s32[]{:T(128)}, f32[4,280,112]{2,1,0:T(8,128)S(1)}, /*index=5*/f32[4]{0:T(1...) while((s32[]{:T(128)}, f32[280,112]{1,0:T(8,128)S(1)}, f32[280]{0:T(512)S(1)}, ...), condition=%wide.region_4.5_spmd.clone, body=%wide.region_3.4_spmd.clone.sunk | while | flops 126565 | bytes 382083 | solution.py:58
  111.5 1.7 collective-permute-start.1
  113.4 6.7 %all-reduce.2 = f32[1120]{0:T(1024)S(1)} all-reduce(f32[1120]{0:T(1024)S(1)} %add_dynamic-update-slice_fusion.1), channel_id=1, replica_groups=mesh['group'=2,'tm'=4,'height'=2,'width'=2] {'height','width'}, use_global_device_ids=true, to_apply=%add.2 | all-reduce | flops 1120 | bytes 8960
  120.5 1.6 fusion.22
  122.2 4.5 %collective-permute-done.2 = f32[280,112]{1,0:T(8,128)S(1)} collective-permute-done((f32[280,112]{1,0:T(8,128)S(1)}, f32[280,112]{1,0:T(8,128)S(1)}, u32[]{:S(2)}, u32[]{:S(2)}) %collective-permute-start.2) | collective-permute-done | bytes 125472 | tf_op jit(solution)/shard_map/ppermute | solution.py:30
  128.0 5.8 %all-reduce.9 = f32[1120]{0:T(1024)S(1)} all-reduce(f32[1120]{0:T(1024)S(1)} %reshape.154), channel_id=9, replica_groups=mesh['group'=2,'tm'=4,'height'=2,'width'=2] {'height','width'}, use_global_device_ids=true, to_apply=%region_7.8.clone | all-reduce | flops 1120 | bytes 8960
  134.0 9.2 %all-reduce.10 = (f32[4]{0:T(128)S(1)}, f32[1120]{0:T(1024)S(1)}) all-reduce(f32[4]{0:T(128)S(1)} %copy-done.8, f32[1120]{0:T(1024)S(1)} %dynamic-slice_dynamic-update-slice_fusion), channel_id=1, replica_groups=mesh['group'=2,'tm'=4,'height'=2,'width'=2] {'tm'}, use_global_device_ids=true, to_apply=%add.3 | all-reduce | flops 1124 | bytes 8992
  145.9 16.6 %all-gather.2 = f32[1120,112]{1,0:T(8,128)S(1)} all-gather(f32[280,112]{1,0:T(8,128)} %reduce-scatter.9.cloned.1.call-done), channel_id=4, replica_groups=mesh['group'=2,'tm'=4,'height'=2,'width'=2] {'tm'}, dimensions={0}, use_global_device_ids=true | all-gather | bytes 627200 | tf_op jit(solution)/shard_map/all_gather | solution.py:46
  162.5 4.1 %while.33 = (s32[]{:T(128)}, f32[280,112]{1,0:T(8,128)S(1)}, f32[280]{0:T(512)S(1)}, s32[]{:T(128)}, f32[4,280,112]{2,1,0:T(8,128)S(1)}, /*index=5*/f32[4]{0:T(1...) while((s32[]{:T(128)}, f32[280,112]{1,0:T(8,128)S(1)}, f32[280]{0:T(512)S(1)}, ...), condition=%wide.region_9.10_spmd.clone, body=%wide.region_8.9_spmd.clone.sunk | while | flops 126565 | bytes 382083 | solution.py:58
  166.7 6.9 %all_gather.58 = f32[1120,112]{1,0:T(8,128)S(1)} all-gather(f32[280,112]{1,0:T(8,128)S(1)} %multiply_add_fusion.1), channel_id=1, replica_groups=mesh['group'=2,'tm'=4,'height'=2,'width'=2] {'height','width'}, dimensions={0}, use_global_device_ids=true | all-gather | bytes 627200 | tf_op jit(solution)/shard_map/all_gather | solution.py:192
  175.9 6.8 %all-reduce.5 = f32[1120]{0:T(1024)S(1)} all-reduce(f32[1120]{0:T(1024)S(1)} %add_dynamic-update-slice_fusion), channel_id=1, replica_groups=mesh['group'=2,'tm'=4,'height'=2,'width'=2] {'height','width'}, use_global_device_ids=true, to_apply=%add.5 | all-reduce | flops 1120 | bytes 8960
  (121 shorter events, 24.8 us)
Async XLA Ops:
  7.2 5.4 %copy-start = (bf16[1,8,16,5632]{3,2,1,0:T(8,128)(2,1)S(1)}, bf16[1,8,16,5632]{3,2,1,0:T(8,128)(2,1)}, u32[]{:S(2)}) copy-start(bf16[1,8,16,5632]{3,2,1,0:T(8,128)(2,1)} %param.16) | copy-start | bytes 4325380
  7.2 83.1 %reduce-scatter.7.cloned.1.call-start = ((), (), s32[]{:S(2)}) async-start(), calls=%async_computation.2 | async-start | bytes 716800
  8.9 11.3 %copy-start.1 = (bf16[1,8,16,1120]{3,2,1,0:T(8,128)(2,1)S(1)}, bf16[1,8,16,1120]{3,2,1,0:T(8,128)(2,1)}, u32[]{:S(2)}) copy-start(bf16[1,8,16,1120]{3,2,1,0:T(8,128)(2,1)} %param.12) | copy-start | bytes 860164
  9.3 24.0 %copy-start.6 = (s32[4]{0:T(128)S(1)}, s32[4]{0:T(128)}, u32[]{:S(2)}) copy-start(s32[4]{0:T(128)} %param.15) | copy-start | bytes 52
  9.3 26.0 %copy-start.10 = (u32[32]{0:T(128)S(1)}, u32[32]{0:T(128)}, u32[]{:S(2)}) copy-start(u32[32]{0:T(128)} %constant.148) | copy-start | bytes 388
  9.3 26.6 %copy-start.7 = (u32[32]{0:T(128)S(1)}, u32[32]{0:T(128)}, u32[]{:S(2)}) copy-start(u32[32]{0:T(128)} %constant.158) | copy-start | bytes 388
  9.4 29.5 %copy-start.5 = (bf16[1,8,16,1120]{3,2,1,0:T(8,128)(2,1)S(1)}, bf16[1,8,16,1120]{3,2,1,0:T(8,128)(2,1)}, u32[]{:S(2)}) copy-start(bf16[1,8,16,1120]{3,2,1,0:T(8,128)(2,1)} %param.11) | copy-start | bytes 860164
  12.5 133.3 %reduce-scatter.9.cloned.1.call-start = ((), (), s32[]{:S(2)}) async-start(), calls=%async_computation.3 | async-start | bytes 716800
  13.4 26.2 %collective-permute-start.3 = (bf16[1,2,16,5632]{3,2,1,0:T(8,128)(2,1)S(1)}, bf16[1,2,16,5632]{3,2,1,0:T(8,128)(2,1)}, u32[]{:S(2)}, u32[]{:S(2)}) collective-permute-start(bf16[1,2,16,5632]{3,2,1,0:T(8,128)(2,1)S(1)} %get-tuple-element.358), channel_id=1, source_target_pairs={{0,2},{1,3},{4,6},{5,7},{8,10},{9,11},{12,14},{13,15},{16,18},{17,... | collective-permute-start | bytes 1081352 | tf_op jit(solution)/shard_map/ppermute | solution.py:66
  19.0 23.1 %collective-permute-start.4 = (bf16[1,2,16,5632]{3,2,1,0:T(8,128)(2,1)}, bf16[1,2,16,5632]{3,2,1,0:T(8,128)(2,1)S(1)}, u32[]{:S(2)}, u32[]{:S(2)}) collective-permute-start(bf16[1,2,16,5632]{3,2,1,0:T(8,128)(2,1)} %get-tuple-element.357), channel_id=1, source_target_pairs={{2,0},{3,1},{6,4},{7,5},{10,8},{11,9},{14,12},{15,13},{18,16},{19,... | collective-permute-start | bytes 1081352 | tf_op jit(solution)/shard_map/ppermute | solution.py:69
  43.3 32.9 %collective-permute-start.5 = (bf16[1,12,2,5632]{3,2,1,0:T(2,128)(2,1)}, bf16[1,12,2,5632]{3,2,1,0:T(2,128)(2,1)}, u32[]{:S(2)}, u32[]{:S(2)}) collective-permute-start(bf16[1,12,2,5632]{3,2,1,0:T(2,128)(2,1)} %get-tuple-element.355), channel_id=1, source_target_pairs={{0,1},{2,3},{4,5},{6,7},{8,9},{10,11},{12,13},{14,15},{16,17},{18,... | collective-permute-start | bytes 811016 | tf_op jit(solution)/shard_map/ppermute | solution.py:66
  47.5 28.8 %collective-permute-start.6 = (bf16[1,12,2,5632]{3,2,1,0:T(2,128)(2,1)}, bf16[1,12,2,5632]{3,2,1,0:T(2,128)(2,1)}, u32[]{:S(2)}, u32[]{:S(2)}) collective-permute-start(bf16[1,12,2,5632]{3,2,1,0:T(2,128)(2,1)} %get-tuple-element.356), channel_id=1, source_target_pairs={{1,0},{3,2},{5,4},{7,6},{9,8},{11,10},{13,12},{15,14},{17,16},{19,... | collective-permute-start | bytes 811016 | tf_op jit(solution)/shard_map/ppermute | solution.py:69
  86.5 20.7 %copy-start.9 = (f32[4]{0:T(128)S(1)}, f32[4]{0:T(128)}, u32[]{:S(2)}) copy-start(f32[4]{0:T(128)} %get-tuple-element.455) | copy-start | bytes 52
  90.3 30.2 %copy-start.2 = (f32[128,10,112]{0,2,1:T(8,128)S(1)}, f32[128,10,112]{0,2,1:T(8,128)}, u32[]{:S(2)}) copy-start(f32[128,10,112]{0,2,1:T(8,128)} %copy.39) | copy-start | bytes 1720324
  90.3 21.1 %copy-start.3 = (f32[280,112]{1,0:T(8,128)S(1)}, f32[280,112]{1,0:T(8,128)}, u32[]{:S(2)}) copy-start(f32[280,112]{1,0:T(8,128)} %reduce-scatter.7.cloned.1.call-done) | copy-start | bytes 376324
  111.4 10.6 %collective-permute-start = (f32[280,112]{1,0:T(8,128)S(1)}, f32[280,112]{1,0:T(8,128)S(1)}, u32[]{:S(2)}, u32[]{:S(2)}) collective-permute-start(f32[280,112]{1,0:T(8,128)S(1)} %get-tuple-element.352), channel_id=1, source_target_pairs={{0,1},{1,2},{2,3},{3,0},{4,5},{5,6},{6,7},{7,4},{8,9},{9,10},{10,1... | collective-permute-start | bytes 376328 | tf_op jit(solution)/shard_map/ppermute | solution.py:30
  111.5 10.7 %collective-permute-start.1 = (f32[280,112]{1,0:T(8,128)S(1)}, f32[280,112]{1,0:T(8,128)S(1)}, u32[]{:S(2)}, u32[]{:S(2)}) collective-permute-start(f32[280,112]{1,0:T(8,128)S(1)} %get-tuple-element.352), channel_id=1, source_target_pairs={{0,3},{1,0},{2,1},{3,2},{4,7},{5,4},{6,5},{7,6},{8,11},{9,8},{10,9... | collective-permute-start | bytes 376328 | tf_op jit(solution)/shard_map/ppermute | solution.py:35
  120.5 13.6 %copy-start.8 = (f32[4]{0:T(128)S(1)}, f32[4]{0:T(128)}, u32[]{:S(2)}) copy-start(f32[4]{0:T(128)} %dynamic-update-slice.3) | copy-start | bytes 52
  122.1 4.6 %collective-permute-start.2 = (f32[280,112]{1,0:T(8,128)S(1)}, f32[280,112]{1,0:T(8,128)S(1)}, u32[]{:S(2)}, u32[]{:S(2)}) collective-permute-start(f32[280,112]{1,0:T(8,128)S(1)} %collective-permute-done), channel_id=1, source_target_pairs={{0,1},{1,2},{2,3},{3,0},{4,5},{5,6},{6,7},{7,4},{8,9},{9,10},{10,1... | collective-permute-start | bytes 376328 | tf_op jit(solution)/shard_map/ppermute | solution.py:30
  145.9 20.8 %copy-start.4 = (f32[280,112]{1,0:T(8,128)S(1)}, f32[280,112]{1,0:T(8,128)}, u32[]{:S(2)}) copy-start(f32[280,112]{1,0:T(8,128)} %reduce-scatter.9.cloned.1.call-done) | copy-start | bytes 376324
Sparse Core Ops, SparseCore 0:
  12.7 24.6 reduce-scatter.6
  122.2 19.7 reduce-scatter.8
